TPU v7x, 32 devices: a whole 2x2x4 slice. The times are simulated.
32 devices in a mesh: seq: 8 (over z, core), tp: 4 (over y, x).
Axes of the slice: x: 2, y: 2, z: 4, core: 2. Of those that a mesh axis runs over, the one named last changes fastest.
Arguments:
- tokens: bfloat16 [64, 6144], P('seq'), may hold values from -6 to 6
- out_grad: bfloat16 [64, 6144], P('seq'), may hold values from -1.5 to 1.5
- w_in: bfloat16 [6144, 24576], P('seq', 'tp'), may hold values from -0.078125 to 0.078125
- w_out: bfloat16 [24576, 6144], P('tp', 'seq'), may hold values from -0.0390625 to 0.0390625
Outputs:
- input_grad: bfloat16 [64, 6144], P('tp', 'seq')
- grad_in: float32 [6144, 24576], P('seq', 'tp')
- grad_out: float32 [24576, 6144], P('tp', 'seq')
All inputs are finite; a program needn't handle non-finite values.
Results may differ from a plain program's by a relative error of at most 0.0051.
Values may be sent and summed in bfloat16 or wider, within the bound.
A program may use at most 128 MiB of HBM per device.

v0:
```python
import jax
import jax.numpy as jnp
from jax import lax
from jax.sharding import PartitionSpec as P


def over_rows(left, right):
    return lax.dot_general(
        left, right, (((0,), (0,)), ((), ())), preferred_element_type=jnp.float32
    )


def over_cols(left, right):
    return lax.dot_general(
        left, right, (((1,), (1,)), ((), ())), preferred_element_type=jnp.float32
    )


def per_device(tokens, out_grad, w_in, w_out):
    cols_x, cols_dy = (
        lax.all_to_all(tokens, "seq", split_axis=1, concat_axis=0, tiled=True),
        lax.all_to_all(out_grad, "seq", split_axis=1, concat_axis=0, tiled=True),
    )
    pre = jnp.dot(cols_x, w_in, preferred_element_type=jnp.float32)
    hidden_grad = over_cols(cols_dy, w_out)
    pre_share, grad_share = (
        lax.psum_scatter(pre, "seq", scatter_dimension=0, tiled=True),
        lax.psum_scatter(hidden_grad, "seq", scatter_dimension=0, tiled=True),
    )
    posit = jnp.maximum(pre_share, 0.0)
    act = (posit * posit).astype(jnp.bfloat16)
    slope = (2.0 * posit * grad_share).astype(jnp.bfloat16)
    act_piece = lax.all_gather(act, "seq", axis=0, tiled=True)
    slope_piece = lax.all_gather(slope, "seq", axis=0, tiled=True)
    sum_out = over_rows(act_piece, cols_dy)
    sum_in = over_rows(cols_x, slope_piece)
    partial_value = over_cols(slope_piece, w_in)
    grad_in, grad_out, partial_value = (sum_in, sum_out, partial_value)
    input_grad = lax.psum_scatter(partial_value, "tp", scatter_dimension=0, tiled=True).astype(
        jnp.bfloat16
    )
    return (input_grad, grad_in, grad_out)


def solution(mesh):
    return jax.shard_map(
        per_device,
        mesh=mesh,
        in_specs=(P("seq", None), P("seq", None), P("seq", "tp"), P("tp", "seq")),
        out_specs=(P("tp", "seq"), P("seq", "tp"), P("tp", "seq")),
        check_vma=False,
    )
```

profile of v0, /device:TPU:0, one launch (start us, length us, event | category | flops | bytes accessed | tf_op | source)
XLA Modules:
  0.0 180.2 jit_solution(3376550464443689663)
XLA Ops:
  7.2 0.0 reduce-scatter.6.cloned.1.call-start
  7.2 12.7 %all_to_all.38 = bf16[8,8,768]{2,0,1:T(8,128)(2,1)S(1)} all-to-all(bf16[8,8,768]{2,0,1:T(8,128)(2,1)} %bitcast.24), channel_id=1, replica_groups=mesh['seq'=8,'tp'=4] {'seq'}, dimensions={1} | all-to-all | bytes 196608 | tf_op jit(solution)/shard_map/all_to_all | solution.py:22
  19.9 0.0 copy-start
  19.9 7.8 %fusion.2 = f32[64,6144]{1,0:T(8,128)} fusion(bf16[6144,768]{1,0:T(8,128)(2,1)} %param.7, bf16[8,8,768]{2,0,1:T(8,128)(2,1)S(1)} %all_to_all.38), kind=kOutput, calls=%fused_computation.5 | convolution fusion | flops 603979776 | bytes 11108352 | tf_op jit(solution)/shard_map/dot_general | solution.py:14
  27.7 0.0 reduce-scatter.6.cloned.1.call-update
  27.7 0.0 reduce-scatter.4.cloned.1.call-start
  27.8 0.0 copy-done
  27.8 8.8 %all_to_all.39 = bf16[8,8,768]{2,0,1:T(8,128)(2,1)S(1)} all-to-all(bf16[8,8,768]{2,0,1:T(8,128)(2,1)S(1)} %bitcast.25), channel_id=1, replica_groups=mesh['seq'=8,'tp'=4] {'seq'}, dimensions={1} | all-to-all | bytes 196608 | tf_op jit(solution)/shard_map/all_to_all | solution.py:21
  36.6 6.6 %fusion.5 = f32[64,6144]{1,0:T(8,128)} fusion(bf16[768,6144]{1,0:T(8,128)(2,1)} %param.6, bf16[8,8,768]{2,0,1:T(8,128)(2,1)S(1)} %all_to_all.39), kind=kOutput, calls=%fused_computation.8 | convolution fusion | flops 603979776 | bytes 11108352 | tf_op jit(solution)/shard_map/dot_general | solution.py:24
  43.2 0.0 reduce-scatter.4.cloned.1.call-update
  43.2 0.0 reduce-scatter.8.cloned.1.call-start
  43.3 17.8 %reduce-scatter.6.cloned.1.call-done = f32[8,6144]{1,0:T(8,128)} async-done(((f32[64,6144]{1,0:T(8,128)}), f32[8,6144]{1,0:T(8,128)}) %reduce-scatter.6.cloned.1.call-update) | async-done | bytes 196624 | tf_op jit(solution)/shard_map/reduce_scatter | solution.py:28
  61.0 35.5 %reduce-scatter.4.cloned.1.call-done = f32[8,6144]{1,0:T(8,128)} async-done(((f32[64,6144]{1,0:T(8,128)}), f32[8,6144]{1,0:T(8,128)}) %reduce-scatter.4.cloned.1.call-update) | async-done | bytes 196624 | tf_op jit(solution)/shard_map/reduce_scatter | solution.py:27
  96.6 1.1 multiply_convert_fusion
  97.6 15.8 %all_gather.7 = bf16[64,6144]{1,0:T(8,128)(2,1)S(1)} all-gather(bf16[8,6144]{1,0:T(8,128)(2,1)S(1)} %get-tuple-element.6), channel_id=1, replica_groups=mesh['seq'=8,'tp'=4] {'seq'}, dimensions={0}, use_global_device_ids=true | all-gather | bytes 884736 | tf_op jit(solution)/shard_map/all_gather | solution.py:33
  113.4 16.2 %all_gather.6 = bf16[64,6144]{1,0:T(8,128)(2,1)S(1)} all-gather(bf16[8,6144]{1,0:T(8,128)(2,1)S(1)} %get-tuple-element.7), channel_id=1, replica_groups=mesh['seq'=8,'tp'=4] {'seq'}, dimensions={0}, use_global_device_ids=true | all-gather | bytes 884736 | tf_op jit(solution)/shard_map/all_gather | solution.py:34
  129.6 7.3 %fusion.7 = f32[64,768]{1,0:T(8,128)} fusion(bf16[64,6144]{1,0:T(8,128)(2,1)S(1)} %all_gather.6, bf16[768,6144]{1,0:T(8,128)(2,1)} %param.6), kind=kOutput, calls=%fused_computation.10 | convolution fusion | flops 603979776 | bytes 10420224 | tf_op jit(solution)/shard_map/dot_general | solution.py:14
  136.9 0.0 reduce-scatter.8.cloned.1.call-update
  137.0 8.3 %convolution_bitcast_fusion = f32[768,6144]{0,1:T(8,128)} fusion(bf16[64,6144]{1,0:T(8,128)(2,1)S(1)} %all_gather.6, bf16[8,8,768]{2,0,1:T(8,128)(2,1)S(1)} %all_to_all.39), kind=kOutput, calls=%fused_computation | convolution fusion | flops 603979776 | bytes 19759104 | tf_op jit(solution)/shard_map/dot_general | solution.py:8
  145.3 18.7 %copy.7 = f32[768,6144]{1,0:T(8,128)} copy(f32[768,6144]{0,1:T(8,128)} %convolution_bitcast_fusion) | data formatting | bytes 37748736
  164.0 8.3 %fusion = f32[6144,768]{1,0:T(8,128)} fusion(bf16[64,6144]{1,0:T(8,128)(2,1)S(1)} %all_gather.7, bf16[8,8,768]{2,0,1:T(8,128)(2,1)S(1)} %all_to_all.38), kind=kOutput, calls=%fused_computation.3 | convolution fusion | flops 603979776 | bytes 19759104 | tf_op jit(solution)/shard_map/dot_general | solution.py:8
  172.2 0.0 reduce-scatter.8.cloned.1.call-done
  172.2 1.4 convert_element_type.10
Async XLA Ops:
  7.2 53.9 %reduce-scatter.6.cloned.1.call-start = ((), (), s32[]{:S(2)}) async-start(), calls=%async_computation.6 | async-start | bytes 1769472 | tf_op jit(solution)/shard_map/reduce_scatter | solution.py:28
  19.9 7.9 %copy-start = (bf16[8,6144]{1,0:T(8,128)(2,1)S(1)}, bf16[8,6144]{1,0:T(8,128)(2,1)}, u32[]{:S(2)}) copy-start(bf16[8,6144]{1,0:T(8,128)(2,1)} %param.4) | copy-start | bytes 294916
  27.7 68.9 %reduce-scatter.4.cloned.1.call-start = ((), (), s32[]{:S(2)}) async-start(), calls=%async_computation.5 | async-start | bytes 1769472 | tf_op jit(solution)/shard_map/reduce_scatter | solution.py:27
  43.2 129.0 %reduce-scatter.8.cloned.1.call-start = ((), (), s32[]{:S(2)}) async-start(), calls=%async_computation.7 | async-start | bytes 245760 | tf_op jit(solution)/shard_map/reduce_scatter | solution.py:39
Sparse Core Ops, SparseCore 0:
  27.8 33.1 reduce-scatter.5
  63.9 32.6 reduce-scatter.3
  137.1 21.8 reduce-scatter.7
where the time goes:
time: 181 us; the launch traced here: 180 us
  blocking collectives  53.5 us (30%)
  waiting for transfers between devices  53.3 us (29%)
  matrix products  38.3 us (21%)
  local copies, waits for them, and re-layouts  18.7 us (10%)
  between operations  13.8 us (8%)
  other arithmetic  2.47 us (1%)
    reduce_scatter x1, waiting for transfers between devices, per_device(): lax.psum_scatter(pre, 'seq', scatter_dimension=0, tiled=True)  35.5 us
    unnamed x3, local copies, waits for them, and re-layouts  18.7 us
    reduce_scatter x1, waiting for transfers between devices, per_device(): lax.psum_scatter(hidden_grad, 'seq', scatter_dimension=0, tiled=True)  17.8 us
    dot_general x2, matrix products, over_rows(): lax.dot_general(left, right, (((0,), (0,)), ((), ())), preferred_element_...  16.6 us
    all_gather x1, blocking collectives, per_device(): slope_piece = lax.all_gather(slope, 'seq', axis=0, tiled=True)  16.2 us
    all_gather x1, blocking collectives, per_device(): act_piece = lax.all_gather(act, 'seq', axis=0, tiled=True)  15.8 us
    dot_general x2, matrix products, over_cols(): lax.dot_general(left, right, (((1,), (1,)), ((), ())), preferred_element_...  15.1 us
    all_to_all x1, blocking collectives, per_device(): lax.all_to_all(out_grad, 'seq', split_axis=1, concat_axis=0, tiled=True)  12.7 us
  transfers between devices with their start and end apart: 3, of which 2 were waited for; matrix products, arithmetic and copies ran while one was open for 23% of the time, Pallas kernels for 0%

commit v1 on v0

--- a/solution.py
+++ b/solution.py
@@ -30,8 +30,11 @@
     posit = jnp.maximum(pre_share, 0.0)
     act = (posit * posit).astype(jnp.bfloat16)
     slope = (2.0 * posit * grad_share).astype(jnp.bfloat16)
-    act_piece = lax.all_gather(act, "seq", axis=0, tiled=True)
-    slope_piece = lax.all_gather(slope, "seq", axis=0, tiled=True)
+    act_piece, slope_piece = jnp.split(
+        lax.all_gather(jnp.concatenate([act, slope], axis=1), "seq", axis=0, tiled=True),
+        [act.shape[1]],
+        axis=1,
+    )
     sum_out = over_rows(act_piece, cols_dy)
     sum_in = over_rows(cols_x, slope_piece)
     partial_value = over_cols(slope_piece, w_in)

time: 181 us -> 173 us (0.956)
  blocking collectives: 53.5 us -> 21.5 us
  waiting for transfers between devices: 53.3 us -> 76.8 us
    all_gather x2 -> x0, blocking collectives: 32 us -> none  [the longest x1 16.2 us: per_device(): slope_piece = lax.all_gather(slope, 'seq', axis=0, tiled=True)]
    all_gather x0 -> x1, waiting for transfers between devices: none -> 23.4 us  [per_device(): lax.all_gather(jnp.concatenate([act, slope], axis=1), 'seq', axis=0, tile...]
    unnamed x3 -> x5, local copies, waits for them, and re-layouts: 18.7 us -> 18.7 us
  transfers between devices with their start and end apart: 3 -> 4, of which waited for: 2 -> 3; matrix products, arithmetic and copies ran while one was open for 23% -> 24% of each run, Pallas kernels for 0% -> 0%
where the time goes in v1:
time: 173 us
  waiting for transfers between devices  76.8 us (44%)
  matrix products  38.7 us (22%)
  blocking collectives  21.5 us (12%)
  local copies, waits for them, and re-layouts  18.7 us (11%)
  between operations  13.8 us (8%)
  other arithmetic  3.16 us (2%)
    reduce_scatter x1, waiting for transfers between devices, per_device(): lax.psum_scatter(pre, 'seq', scatter_dimension=0, tiled=True)  35.5 us
    all_gather x1, waiting for transfers between devices, per_device(): lax.all_gather(jnp.concatenate([act, slope], axis=1), 'seq', axis=0, tile...  23.4 us
    unnamed x5, local copies, waits for them, and re-layouts  18.7 us
    reduce_scatter x1, waiting for transfers between devices, per_device(): lax.psum_scatter(hidden_grad, 'seq', scatter_dimension=0, tiled=True)  17.8 us
    dot_general x2, matrix products, over_rows(): lax.dot_general(left, right, (((0,), (0,)), ((), ())), preferred_element_...  16.6 us
    dot_general x2, matrix products, over_cols(): lax.dot_general(left, right, (((1,), (1,)), ((), ())), preferred_element_...  15.5 us
    all_to_all x1, blocking collectives, per_device(): lax.all_to_all(out_grad, 'seq', split_axis=1, concat_axis=0, tiled=True)  12.7 us
    all_to_all x1, blocking collectives, per_device(): lax.all_to_all(tokens, 'seq', split_axis=1, concat_axis=0, tiled=True)  8.8 us
  transfers between devices with their start and end apart: 4, of which 3 were waited for; matrix products, arithmetic and copies ran while one was open for 24% of the time, Pallas kernels for 0%

profile of v1, /device:TPU:0, one launch (start us, length us, event | category | flops | bytes accessed | tf_op | source)
XLA Modules:
  0.0 172.8 jit_solution(10606730454432628950)
XLA Ops:
  7.2 0.0 reduce-scatter.6.cloned.1.call-start
  7.2 12.7 %all_to_all.38 = bf16[8,8,768]{2,0,1:T(8,128)(2,1)S(1)} all-to-all(bf16[8,8,768]{2,0,1:T(8,128)(2,1)} %bitcast.21), channel_id=1, replica_groups=mesh['seq'=8,'tp'=4] {'seq'}, dimensions={1} | all-to-all | bytes 196608 | tf_op jit(solution)/shard_map/all_to_all | solution.py:22
  19.9 7.8 %fusion.6 = f32[64,6144]{1,0:T(8,128)} fusion(bf16[6144,768]{1,0:T(8,128)(2,1)} %param.7, bf16[8,8,768]{2,0,1:T(8,128)(2,1)S(1)} %all_to_all.38), kind=kOutput, calls=%fused_computation.10 | convolution fusion | flops 603979776 | bytes 11108352 | tf_op jit(solution)/shard_map/dot_general | solution.py:14
  27.7 0.0 reduce-scatter.6.cloned.1.call-update
  27.7 0.0 reduce-scatter.4.cloned.1.call-start
  27.8 0.0 copy-done.1
  27.8 8.8 %all_to_all.39 = bf16[8,8,768]{2,0,1:T(8,128)(2,1)S(1)} all-to-all(bf16[8,8,768]{2,0,1:T(8,128)(2,1)S(1)} %bitcast.22), channel_id=1, replica_groups=mesh['seq'=8,'tp'=4] {'seq'}, dimensions={1} | all-to-all | bytes 196608 | tf_op jit(solution)/shard_map/all_to_all | solution.py:21
  36.6 6.6 %fusion.9 = f32[64,6144]{1,0:T(8,128)} fusion(bf16[768,6144]{1,0:T(8,128)(2,1)} %param.6, bf16[8,8,768]{2,0,1:T(8,128)(2,1)S(1)} %all_to_all.39), kind=kOutput, calls=%fused_computation.13 | convolution fusion | flops 603979776 | bytes 11108352 | tf_op jit(solution)/shard_map/dot_general | solution.py:24
  43.2 0.0 reduce-scatter.4.cloned.1.call-update
  43.2 0.0 all-gather.2.cloned.1.call-start
  43.3 17.8 %reduce-scatter.6.cloned.1.call-done = f32[8,6144]{1,0:T(8,128)} async-done(((f32[64,6144]{1,0:T(8,128)}), f32[8,6144]{1,0:T(8,128)}) %reduce-scatter.6.cloned.1.call-update) | async-done | bytes 196624 | tf_op jit(solution)/shard_map/reduce_scatter | solution.py:28
  61.0 35.5 %reduce-scatter.4.cloned.1.call-done = f32[8,6144]{1,0:T(8,128)} async-done(((f32[64,6144]{1,0:T(8,128)}), f32[8,6144]{1,0:T(8,128)}) %reduce-scatter.4.cloned.1.call-update) | async-done | bytes 196624 | tf_op jit(solution)/shard_map/reduce_scatter | solution.py:27
  96.6 1.1 multiply_convert_fusion.1
  97.6 0.7 pad_maximum_fusion
  98.3 0.0 all-gather.2.cloned.1.call-update
  98.3 0.0 reduce-scatter.8.cloned.1.call-start
  98.4 23.4 %all-gather.2.cloned.1.call-done = bf16[64,12288]{1,0:T(8,128)(2,1)} async-done(((bf16[8,12288]{1,0:T(8,128)(2,1)}), bf16[64,12288]{1,0:T(8,128)(2,1)}) %all-gather.2.cloned.1.call-update) | async-done | bytes 1572880 | tf_op jit(solution)/shard_map/all_gather | solution.py:34
  121.8 7.7 %fusion.3 = f32[64,768]{1,0:T(8,128)} fusion(bf16[768,6144]{1,0:T(8,128)(2,1)} %param.6, bf16[64,12288]{1,0:T(8,128)(2,1)} %all-gather.2.cloned.1.call-done), kind=kOutput, calls=%fused_computation.4 | convolution fusion | flops 603979776 | bytes 10420224 | tf_op jit(solution)/shard_map/dot_general | solution.py:14
  129.5 0.0 reduce-scatter.8.cloned.1.call-update
  129.6 0.0 copy-done
  129.6 8.3 %convolution_bitcast_fusion = f32[768,6144]{0,1:T(8,128)} fusion(bf16[64,12288]{1,0:T(8,128)(2,1)S(1)} %copy-done, bf16[8,8,768]{2,0,1:T(8,128)(2,1)S(1)} %all_to_all.39), kind=kOutput, calls=%fused_computation | convolution fusion | flops 603979776 | bytes 19759104 | tf_op jit(solution)/shard_map/dot_general | solution.py:8
  137.9 18.7 %copy.7 = f32[768,6144]{1,0:T(8,128)} copy(f32[768,6144]{0,1:T(8,128)} %convolution_bitcast_fusion) | data formatting | bytes 37748736
  156.5 8.3 %fusion = f32[6144,768]{1,0:T(8,128)} fusion(bf16[64,12288]{1,0:T(8,128)(2,1)S(1)} %copy-done, bf16[8,8,768]{2,0,1:T(8,128)(2,1)S(1)} %all_to_all.38), kind=kOutput, calls=%fused_computation.1 | convolution fusion | flops 603979776 | bytes 19759104 | tf_op jit(solution)/shard_map/dot_general | solution.py:8
  164.8 1.4 convert_element_type.11
  (3 shorter events, 0.0 us)
Async XLA Ops:
  7.2 53.9 %reduce-scatter.6.cloned.1.call-start = ((), (), s32[]{:S(2)}) async-start(), calls=%async_computation.6 | async-start | bytes 1769472 | tf_op jit(solution)/shard_map/reduce_scatter | solution.py:28
  19.9 7.9 %copy-start.1 = (bf16[8,6144]{1,0:T(8,128)(2,1)S(1)}, bf16[8,6144]{1,0:T(8,128)(2,1)}, u32[]{:S(2)}) copy-start(bf16[8,6144]{1,0:T(8,128)(2,1)} %param.4) | copy-start | bytes 294916
  27.7 68.9 %reduce-scatter.4.cloned.1.call-start = ((), (), s32[]{:S(2)}) async-start(), calls=%async_computation.5 | async-start | bytes 1769472 | tf_op jit(solution)/shard_map/reduce_scatter | solution.py:27
  43.2 78.6 %all-gather.2.cloned.1.call-start = ((), (), s32[]{:S(2)}) async-start(), calls=%async_computation.7 | async-start | bytes 1769472 | tf_op jit(solution)/shard_map/all_gather | solution.py:34
  98.3 66.5 %reduce-scatter.8.cloned.1.call-start = ((), (), s32[]{:S(2)}) async-start(), calls=%async_computation.8 | async-start | bytes 245760 | tf_op jit(solution)/shard_map/reduce_scatter | solution.py:42
  121.8 7.7 %copy-start = (bf16[64,12288]{1,0:T(8,128)(2,1)S(1)}, bf16[64,12288]{1,0:T(8,128)(2,1)}, u32[]{:S(2)}) copy-start(bf16[64,12288]{1,0:T(8,128)(2,1)} %all-gather.2.cloned.1.call-done) | copy-start | bytes 4718596
Sparse Core Ops, SparseCore 0:
  27.8 33.1 reduce-scatter.5
  63.9 32.6 reduce-scatter.3
  98.8 23.0 all-gather.1
  129.7 23.5 reduce-scatter.7

commit v2 on v0

--- a/solution.py
+++ b/solution.py
@@ -19,7 +19,12 @@
 def per_device(tokens, out_grad, w_in, w_out):
     cols_x, cols_dy = (
         lax.all_to_all(tokens, "seq", split_axis=1, concat_axis=0, tiled=True),
-        lax.all_to_all(out_grad, "seq", split_axis=1, concat_axis=0, tiled=True),
+        jnp.concatenate(
+            lax.all_to_all(
+                jnp.stack(jnp.split(out_grad, lax.axis_size("seq"), axis=1)), "seq", 0, 0
+            ),
+            axis=0,
+        ),
     )
     pre = jnp.dot(cols_x, w_in, preferred_element_type=jnp.float32)
     hidden_grad = over_cols(cols_dy, w_out)

time: 181 us -> 186 us (1.028)
  local copies, waits for them, and re-layouts: 18.7 us -> 24.4 us
    unnamed x3 -> x10, local copies, waits for them, and re-layouts: 18.7 us -> 23.7 us
where the time goes in v2:
time: 186 us
  blocking collectives  53.2 us (29%)
  waiting for transfers between devices  53.2 us (29%)
  matrix products  38.3 us (21%)
  local copies, waits for them, and re-layouts  24.4 us (13%)
  between operations  13.8 us (7%)
  other arithmetic  2.47 us (1%)
    reduce_scatter x1, waiting for transfers between devices, per_device(): lax.psum_scatter(pre, 'seq', scatter_dimension=0, tiled=True)  35.4 us
    unnamed x10, local copies, waits for them, and re-layouts  23.7 us
    reduce_scatter x1, waiting for transfers between devices, per_device(): lax.psum_scatter(hidden_grad, 'seq', scatter_dimension=0, tiled=True)  17.7 us
    dot_general x2, matrix products, over_rows(): lax.dot_general(left, right, (((0,), (0,)), ((), ())), preferred_element_...  16.6 us
    all_gather x1, blocking collectives, per_device(): slope_piece = lax.all_gather(slope, 'seq', axis=0, tiled=True)  16.2 us
    all_gather x1, blocking collectives, per_device(): act_piece = lax.all_gather(act, 'seq', axis=0, tiled=True)  15.8 us
    dot_general x2, matrix products, over_cols(): lax.dot_general(left, right, (((1,), (1,)), ((), ())), preferred_element_...  15.1 us
    all_to_all x1, blocking collectives, per_device(): lax.all_to_all(jnp.stack(jnp.split(out_grad, lax.axis_size('seq'), axis=1...  12.5 us
  transfers between devices with their start and end apart: 3, of which 2 were waited for; matrix products, arithmetic and copies ran while one was open for 23% of the time, Pallas kernels for 0%

profile of v2, /device:TPU:0, one launch (start us, length us, event | category | flops | bytes accessed | tf_op | source)
XLA Modules:
  0.0 185.5 jit_solution(11296879922567359979)
XLA Ops:
  7.2 0.7 constant_dynamic-update-slice_fusion.7
  7.9 0.7 constant_dynamic-update-slice_fusion.6
  8.6 0.7 constant_dynamic-update-slice_fusion.5
  9.3 0.7 constant_dynamic-update-slice_fusion.4
  10.1 0.7 constant_dynamic-update-slice_fusion.3
  10.8 0.7 constant_dynamic-update-slice_fusion.2
  11.5 0.7 constant_dynamic-update-slice_fusion.1
  12.2 0.7 constant_dynamic-update-slice_fusion
  12.9 12.5 %all_to_all.24 = bf16[8,8,768]{2,1,0:T(8,128)(2,1)S(1)} all-to-all(bf16[8,8,768]{2,1,0:T(8,128)(2,1)S(1)} %constant_dynamic-update-slice_fusion), channel_id=1, replica_groups=mesh['seq'=8,'tp'=4] {'seq'}, dimensions={0} | all-to-all | bytes 196608 | tf_op jit(solution)/shard_map/all_to_all | solution.py:23
  25.4 7.8 %fusion.5 = f32[64,6144]{1,0:T(8,128)} fusion(bf16[6144,768]{1,0:T(8,128)(2,1)} %param.7, bf16[8,8,768]{2,1,0:T(8,128)(2,1)S(1)} %all_to_all.24), kind=kOutput, calls=%fused_computation.8 | convolution fusion | flops 603979776 | bytes 11108352 | tf_op jit(solution)/shard_map/dot_general | solution.py:14
  33.2 0.0 reduce-scatter.4.cloned.1.call-start
  33.2 8.8 %all_to_all.25 = bf16[8,8,768]{2,0,1:T(8,128)(2,1)S(1)} all-to-all(bf16[8,8,768]{2,0,1:T(8,128)(2,1)S(1)} %bitcast.37), channel_id=1, replica_groups=mesh['seq'=8,'tp'=4] {'seq'}, dimensions={1} | all-to-all | bytes 196608 | tf_op jit(solution)/shard_map/all_to_all | solution.py:21
  42.0 6.6 %fusion.1 = f32[64,6144]{1,0:T(8,128)} fusion(bf16[768,6144]{1,0:T(8,128)(2,1)} %param.6, bf16[8,8,768]{2,0,1:T(8,128)(2,1)S(1)} %all_to_all.25), kind=kOutput, calls=%fused_computation.4 | convolution fusion | flops 603979776 | bytes 11108352 | tf_op jit(solution)/shard_map/dot_general | solution.py:29
  48.7 0.0 reduce-scatter.8.cloned.1.call-start
  48.8 17.7 %reduce-scatter.6.cloned.1.call-done = f32[8,6144]{1,0:T(8,128)} async-done(((f32[64,6144]{1,0:T(8,128)}), f32[8,6144]{1,0:T(8,128)}) %reduce-scatter.6.cloned.1.call-update) | async-done | bytes 196624 | tf_op jit(solution)/shard_map/reduce_scatter | solution.py:33
  66.5 35.4 %reduce-scatter.4.cloned.1.call-done = f32[8,6144]{1,0:T(8,128)} async-done(((f32[64,6144]{1,0:T(8,128)}), f32[8,6144]{1,0:T(8,128)}) %reduce-scatter.4.cloned.1.call-update) | async-done | bytes 196624 | tf_op jit(solution)/shard_map/reduce_scatter | solution.py:32
  101.9 1.1 multiply_convert_fusion
  103.0 15.8 %all_gather.7 = bf16[64,6144]{1,0:T(8,128)(2,1)S(1)} all-gather(bf16[8,6144]{1,0:T(8,128)(2,1)S(1)} %get-tuple-element.6), channel_id=1, replica_groups=mesh['seq'=8,'tp'=4] {'seq'}, dimensions={0}, use_global_device_ids=true | all-gather | bytes 884736 | tf_op jit(solution)/shard_map/all_gather | solution.py:38
  118.8 16.2 %all_gather.6 = bf16[64,6144]{1,0:T(8,128)(2,1)S(1)} all-gather(bf16[8,6144]{1,0:T(8,128)(2,1)S(1)} %get-tuple-element.7), channel_id=1, replica_groups=mesh['seq'=8,'tp'=4] {'seq'}, dimensions={0}, use_global_device_ids=true | all-gather | bytes 884736 | tf_op jit(solution)/shard_map/all_gather | solution.py:39
  135.0 7.3 %fusion.7 = f32[64,768]{1,0:T(8,128)} fusion(bf16[64,6144]{1,0:T(8,128)(2,1)S(1)} %all_gather.6, bf16[768,6144]{1,0:T(8,128)(2,1)} %param.6), kind=kOutput, calls=%fused_computation.18 | convolution fusion | flops 603979776 | bytes 10420224 | tf_op jit(solution)/shard_map/dot_general | solution.py:14
  142.3 8.3 %convolution_bitcast_fusion = f32[768,6144]{0,1:T(8,128)} fusion(bf16[64,6144]{1,0:T(8,128)(2,1)S(1)} %all_gather.6, bf16[8,8,768]{2,0,1:T(8,128)(2,1)S(1)} %all_to_all.25), kind=kOutput, calls=%fused_computation | convolution fusion | flops 603979776 | bytes 19759104 | tf_op jit(solution)/shard_map/dot_general | solution.py:8
  150.6 18.7 %copy.7 = f32[768,6144]{1,0:T(8,128)} copy(f32[768,6144]{0,1:T(8,128)} %convolution_bitcast_fusion) | data formatting | bytes 37748736
  169.3 8.3 %fusion.3 = f32[6144,768]{1,0:T(8,128)} fusion(bf16[64,6144]{1,0:T(8,128)(2,1)S(1)} %all_gather.7, bf16[8,8,768]{2,1,0:T(8,128)(2,1)S(1)} %all_to_all.24), kind=kOutput, calls=%fused_computation.6 | convolution fusion | flops 603979776 | bytes 19759104 | tf_op jit(solution)/shard_map/dot_general | solution.py:8
  177.6 1.4 convert_element_type.10
  (7 shorter events, 0.1 us)
Async XLA Ops:
  7.2 59.3 %reduce-scatter.6.cloned.1.call-start = ((), (), s32[]{:S(2)}) async-start(), calls=%async_computation.6 | async-start | bytes 1769472 | tf_op jit(solution)/shard_map/reduce_scatter | solution.py:33
  25.4 7.9 %copy-start = (bf16[8,6144]{1,0:T(8,128)(2,1)S(1)}, bf16[8,6144]{1,0:T(8,128)(2,1)}, u32[]{:S(2)}) copy-start(bf16[8,6144]{1,0:T(8,128)(2,1)} %param.4) | copy-start | bytes 294916
  33.2 68.8 %reduce-scatter.4.cloned.1.call-start = ((), (), s32[]{:S(2)}) async-start(), calls=%async_computation.5 | async-start | bytes 1769472 | tf_op jit(solution)/shard_map/reduce_scatter | solution.py:32
  48.7 128.9 %reduce-scatter.8.cloned.1.call-start = ((), (), s32[]{:S(2)}) async-start(), calls=%async_computation.7 | async-start | bytes 245760 | tf_op jit(solution)/shard_map/reduce_scatter | solution.py:44
Sparse Core Ops, SparseCore 0:
  33.3 33.1 reduce-scatter.5
  69.4 32.5 reduce-scatter.3
  142.4 22.1 reduce-scatter.7
